TPU v7x, 256 devices: a whole 4x4x8 slice. The times are simulated.
256 devices in a mesh: dp: 32 (over y_lo, z, core), ctx: 8 (over y_hi, x).
Axes of the slice: x: 4, y: 4 (y_hi: 2, y_lo: 2; y = y_hi * 2 + y_lo), z: 8, core: 2. Of those that a mesh axis runs over, the one named last changes fastest.
Arguments:
- normed_input: bfloat16 [32768, 4096], P(('dp', 'ctx')), may hold values from -24 to 24
- queries: bfloat16 [32768, 4096], P(('dp', 'ctx')), may hold values from -120 to 120
- saved_keys: bfloat16 [32768, 512], P(('dp', 'ctx')), may hold values from -6 to 6
- saved_values: bfloat16 [32768, 512], P(('dp', 'ctx')), may hold values from -6 to 6
- attention_output: bfloat16 [32768, 4096], P(('dp', 'ctx')), may hold values from -6 to 6, as said below
- saved_log_totals: float32 [32768, 32], P(('dp', 'ctx')), as said below
- output_gradient: bfloat16 [32768, 4096], P(('dp', 'ctx')), may hold values from -6 to 6
- document_lengths: int32 [32, 4], P('dp'), may hold values from 1 to 512, as said below
Outputs:
- query_gradient: bfloat16 [32768, 4096], P(('dp', 'ctx'))
- key_weight_grad: float32 [4096, 512], P(('dp', 'ctx'))
- value_weight_grad: float32 [4096, 512], P(('dp', 'ctx'))
Inputs may be any that keep to these rules, and one draw needn't show every extreme that they name: `document_lengths`: each sequence holds 4 documents whose lengths sum to 1024; the longest is exactly 512. attention_output is the forward's output, the softmax over allowed keys of the scores applied to saved_values, for the given queries, saved_keys, saved_values and document_lengths, rounded to bfloat16. saved_log_totals is the log of the sum of exp of the allowed scores of each query row and head, for the given queries, saved_keys and document_lengths.
All inputs are finite; a program needn't handle non-finite values.
Results may differ from a plain program's by a relative error of at most 0.0051.
Values may be sent and summed in bfloat16 or wider, within the bound.
A program may use at most 128 MiB of HBM per device.

v0:
```python
import math

import jax
import jax.numpy as jnp
from jax import lax
from jax.sharding import PartitionSpec as P

QUERY_HEADS = 32
KEY_VALUE_HEADS = 4
HEAD_SIZE = 128


def shifted(value, axis, steps):
    count = lax.axis_size(axis)
    pairs = [(source, (source + steps) % count) for source in range(count)]
    return lax.ppermute(value, axis, pairs)


def doc_of(doc_ends, positions):
    return jnp.sum((doc_ends[None, :] <= positions[:, None]).astype(jnp.int32), axis=1)


def local(
    normed_input,
    queries,
    saved_keys,
    saved_values,
    attention_output,
    saved_log_totals,
    output_gradient,
    document_lengths,
):
    token_rows = queries.shape[0]
    key_value_width = saved_keys.shape[1]
    group_count = QUERY_HEADS // KEY_VALUE_HEADS
    ctx_count = lax.axis_size("ctx")
    ctx_rank = lax.axis_index("ctx")
    softmax_scale = 1.0 / math.sqrt(HEAD_SIZE)
    doc_ends = jnp.cumsum(document_lengths[0])
    local_ids = jnp.arange(token_rows, dtype=jnp.int32)
    query_pos = local_ids * ctx_count + ctx_rank
    query_doc = doc_of(doc_ends, query_pos)
    query_tensor_four = queries.reshape(token_rows, KEY_VALUE_HEADS, group_count, HEAD_SIZE)
    output_gradient_four = output_gradient.reshape(
        token_rows, KEY_VALUE_HEADS, group_count, HEAD_SIZE
    )
    key_value = jnp.concatenate([saved_keys, saved_values], axis=1)
    log_softmax_total = jnp.transpose(
        saved_log_totals.reshape(token_rows, KEY_VALUE_HEADS, group_count), (1, 2, 0)
    )
    product_rows = output_gradient_four.astype(jnp.float32) * attention_output.reshape(
        token_rows, KEY_VALUE_HEADS, group_count, HEAD_SIZE
    ).astype(jnp.float32)
    delta_row = jnp.transpose(jnp.sum(product_rows, axis=-1), (1, 2, 0))

    def block_mask(first_row, block_rows):
        key_ids = first_row + jnp.arange(block_rows, dtype=jnp.int32)
        key_pos = key_ids % token_rows * ctx_count + key_ids // token_rows
        key_doc = doc_of(doc_ends, key_pos)
        return (query_doc[:, None] == key_doc[None, :]) & (key_pos[None, :] <= query_pos[:, None])

    def backward_block(key_block_slice, first_row, grad_block, query_grad):
        allowed = block_mask(first_row, key_block_slice.shape[0])
        key_tensor_three = key_block_slice[:, :key_value_width].reshape(
            -1, KEY_VALUE_HEADS, HEAD_SIZE
        )
        value_tensor_three = key_block_slice[:, key_value_width:].reshape(
            -1, KEY_VALUE_HEADS, HEAD_SIZE
        )
        score_matrix = (
            jnp.einsum(
                "szot,mzt->zosm",
                query_tensor_four,
                key_tensor_three,
                preferred_element_type=jnp.float32,
            )
            * softmax_scale
        )
        probs = jnp.where(allowed, jnp.exp(score_matrix - log_softmax_total[..., None]), 0.0)
        grad_probs = jnp.einsum(
            "szot,mzt->zosm",
            output_gradient_four,
            value_tensor_three,
            preferred_element_type=jnp.float32,
        )
        grad_scores = (probs * (grad_probs - delta_row[..., None])).astype(jnp.bfloat16)
        probs_low = probs.astype(jnp.bfloat16)
        query_grad = query_grad + jnp.einsum(
            "sjba,asp->bsjp", grad_scores, key_tensor_three, preferred_element_type=jnp.float32
        )
        key_part = (
            jnp.einsum(
                "hgqk,qhgd->khd", grad_scores, query_tensor_four, preferred_element_type=jnp.float32
            )
            * softmax_scale
        )
        value_part = jnp.einsum(
            "hgqk,qhgd->khd", probs_low, output_gradient_four, preferred_element_type=jnp.float32
        )
        block_rows = key_block_slice.shape[0]
        grad_block = grad_block + jnp.concatenate(
            [
                key_part.reshape(block_rows, key_value_width),
                value_part.reshape(block_rows, key_value_width),
            ],
            axis=1,
        )
        return (grad_block, query_grad)

    def send_grads(grad_block):
        return shifted(grad_block, "ctx", 1)

    grad_block, query_grad = backward_block(
        key_value,
        ctx_rank * token_rows,
        jnp.zeros((token_rows, 2 * key_value_width), jnp.float32),
        jnp.zeros((token_rows, KEY_VALUE_HEADS, group_count, HEAD_SIZE), jnp.float32),
    )

    def backward_step(step_index, state):
        visiting, grad_now, query_now = state
        visiting = shifted(visiting, "ctx", 1)
        grad_now = send_grads(grad_now)
        owner = (ctx_rank - step_index) % ctx_count
        grad_now, query_now = backward_block(visiting, owner * token_rows, grad_now, query_now)
        return (visiting, grad_now, query_now)

    finished = lax.fori_loop(1, ctx_count, backward_step, (key_value, grad_block, query_grad))
    grad_block = send_grads(finished[1])
    query_gradient = (
        (finished[2] * softmax_scale)
        .reshape(token_rows, QUERY_HEADS * HEAD_SIZE)
        .astype(jnp.bfloat16)
    )
    key_grads_low = grad_block.astype(jnp.bfloat16)
    weight_gradient = lax.psum_scatter(
        lax.dot_general(
            normed_input,
            key_grads_low,
            (((0,), (0,)), ((), ())),
            preferred_element_type=jnp.float32,
        ),
        ("dp", "ctx"),
        scatter_dimension=0,
        tiled=True,
    )
    return (
        query_gradient,
        weight_gradient[:, :key_value_width],
        weight_gradient[:, key_value_width:],
    )


def solution(mesh):
    placed = (
        P(("dp", "ctx"), None),
        P(("dp", "ctx"), None),
        P(("dp", "ctx"), None),
        P(("dp", "ctx"), None),
        P(("dp", "ctx"), None),
        P(("dp", "ctx"), None),
        P(("dp", "ctx"), None),
        P("dp", None),
    )
    return jax.shard_map(
        local,
        mesh=mesh,
        in_specs=placed,
        out_specs=(P(("dp", "ctx"), None), P(("dp", "ctx"), None), P(("dp", "ctx"), None)),
        check_vma=False,
    )
```

profile of v0, /device:TPU:128, one launch (start us, length us, event | category | flops | bytes accessed | tf_op | source)
XLA Modules:
  0.0 1561.5 jit_solution(7562466668035430436)
XLA Ops:
  8.2 1.7 copy.86
  10.9 1.7 copy.87
  13.4 1.6 copy.91
  15.0 1.6 copy.88
  16.6 2.6 copy.94
  19.4 1.9 multiply_reduce_fusion
  23.3 1.9 convolution_bitcast_fusion.2
  26.7 157.0 %while.22 = (s32[]{:T(128)}, bf16[128,1024]{0,1:T(8,128)(2,1)}, f32[128,1024]{0,1:T(8,128)}, f32[128,4,8,128]{3,0,2,1:T(8,128)}, s32[128]{0:T(128)S(1)}, /*index...) while((s32[]{:T(128)}, bf16[128,1024]{0,1:T(8,128)(2,1)}, ...), condition=%wide.region_6.7_spmd.clone.clone, body=%wide.region_4.6_spmd.clone.clone.sunk | while | flops 675664256 | bytes 41357752 | solution.py:128
  29.9 9.8 collective-permute-done
  44.0 5.9 collective-permute-done.1
  49.9 1.9 maximum_add_fusion.2
  52.1 12.8 collective-permute-done
  69.2 5.0 collective-permute-done.1
  74.2 1.9 maximum_add_fusion.2
  76.4 12.8 collective-permute-done
  93.5 4.1 collective-permute-done.1
  97.6 1.9 maximum_add_fusion.2
  99.8 12.8 collective-permute-done
  116.9 3.2 collective-permute-done.1
  120.0 1.9 maximum_add_fusion.2
  122.2 12.8 collective-permute-done
  139.3 2.3 collective-permute-done.1
  141.6 1.9 maximum_add_fusion.2
  143.7 12.7 collective-permute-done
  162.2 1.9 maximum_add_fusion.2
  164.3 11.7 collective-permute-done
  181.8 1.9 maximum_add_fusion.2
  185.0 10.0 collective-permute-done.2
  195.0 8.0 convolution_bitcast_fusion.1
  203.0 17.5 %copy.134 = f32[4096,1024]{1,0:T(8,128)} copy(f32[4096,1024]{0,1:T(8,128)} %convolution_bitcast_fusion.1) | data formatting | bytes 33554432
  220.5 1.6 copy-done.3
  224.5 1328.8 %reduce-scatter.4.cloned.1.call-done = f32[16,1024]{1,0:T(8,128)} async-done(((f32[4096,1024]{1,0:T(8,128)}), f32[16,1024]{1,0:T(8,128)}) %reduce-scatter.4.cloned.1.call-update) | async-done | bytes 65552
  (150 shorter events, 48.6 us)
Async XLA Ops:
  7.2 187.8 %copy-start = (bf16[128,4096]{1,0:T(8,128)(2,1)S(1)}, bf16[128,4096]{1,0:T(8,128)(2,1)}, u32[]{:S(2)}) copy-start(bf16[128,4096]{1,0:T(8,128)(2,1)} %param.10) | copy-start | bytes 3145732
  7.2 1546.1 %reduce-scatter.4.cloned.1.call-start = ((), (), s32[]{:S(2)}) async-start(), calls=%async_computation.1 | async-start | bytes 16842752
  19.2 2.1 copy-start.4
  23.3 1.9 copy-start.5
  23.3 1.9 copy-start.6
  26.7 13.0 collective-permute-start
  28.2 21.7 %collective-permute-start.1 = (f32[128,1024]{0,1:T(8,128)}, f32[128,1024]{0,1:T(8,128)}, u32[]{:S(2)}, u32[]{:S(2)}) collective-permute-start(f32[128,1024]{0,1:T(8,128)} %get-tuple-element.518), channel_id=1, source_target_pairs={{0,1},{1,2},{2,3},{3,4},{4,5},{5,6},{6,7},{7,0},{8,9},{9,10},{10,1... | collective-permute-start | bytes 1572872 | tf_op jit(solution)/shard_map/while/body/eval_jaxpr/ppermute | solution.py:16
  41.3 1.7 copy-start.1
  44.0 7.9 copy-start.2
  51.8 13.1 collective-permute-start
  51.8 22.4 %collective-permute-start.1 = (f32[128,1024]{0,1:T(8,128)}, f32[128,1024]{0,1:T(8,128)}, u32[]{:S(2)}, u32[]{:S(2)}) collective-permute-start(f32[128,1024]{0,1:T(8,128)} %get-tuple-element.518), channel_id=1, source_target_pairs={{0,1},{1,2},{2,3},{3,4},{4,5},{5,6},{6,7},{7,0},{8,9},{9,10},{10,1... | collective-permute-start | bytes 1572872 | tf_op jit(solution)/shard_map/while/body/eval_jaxpr/ppermute | solution.py:16
  66.5 1.7 copy-start.1
  69.2 7.0 copy-start.2
  76.1 13.1 collective-permute-start
  76.1 21.5 %collective-permute-start.1 = (f32[128,1024]{0,1:T(8,128)}, f32[128,1024]{0,1:T(8,128)}, u32[]{:S(2)}, u32[]{:S(2)}) collective-permute-start(f32[128,1024]{0,1:T(8,128)} %get-tuple-element.518), channel_id=1, source_target_pairs={{0,1},{1,2},{2,3},{3,4},{4,5},{5,6},{6,7},{7,0},{8,9},{9,10},{10,1... | collective-permute-start | bytes 1572872 | tf_op jit(solution)/shard_map/while/body/eval_jaxpr/ppermute | solution.py:16
  90.8 1.7 copy-start.1
  93.5 6.0 copy-start.2
  99.5 13.1 collective-permute-start
  99.5 20.5 %collective-permute-start.1 = (f32[128,1024]{0,1:T(8,128)}, f32[128,1024]{0,1:T(8,128)}, u32[]{:S(2)}, u32[]{:S(2)}) collective-permute-start(f32[128,1024]{0,1:T(8,128)} %get-tuple-element.518), channel_id=1, source_target_pairs={{0,1},{1,2},{2,3},{3,4},{4,5},{5,6},{6,7},{7,0},{8,9},{9,10},{10,1... | collective-permute-start | bytes 1572872 | tf_op jit(solution)/shard_map/while/body/eval_jaxpr/ppermute | solution.py:16
  114.2 1.7 copy-start.1
  116.8 5.1 copy-start.2
  122.0 13.1 collective-permute-start
  122.0 19.6 %collective-permute-start.1 = (f32[128,1024]{0,1:T(8,128)}, f32[128,1024]{0,1:T(8,128)}, u32[]{:S(2)}, u32[]{:S(2)}) collective-permute-start(f32[128,1024]{0,1:T(8,128)} %get-tuple-element.518), channel_id=1, source_target_pairs={{0,1},{1,2},{2,3},{3,4},{4,5},{5,6},{6,7},{7,0},{8,9},{9,10},{10,1... | collective-permute-start | bytes 1572872 | tf_op jit(solution)/shard_map/while/body/eval_jaxpr/ppermute | solution.py:16
  136.6 1.7 copy-start.1
  139.3 4.2 copy-start.2
  143.5 13.0 collective-permute-start
  143.5 18.7 %collective-permute-start.1 = (f32[128,1024]{0,1:T(8,128)}, f32[128,1024]{0,1:T(8,128)}, u32[]{:S(2)}, u32[]{:S(2)}) collective-permute-start(f32[128,1024]{0,1:T(8,128)} %get-tuple-element.518), channel_id=1, source_target_pairs={{0,1},{1,2},{2,3},{3,4},{4,5},{5,6},{6,7},{7,0},{8,9},{9,10},{10,1... | collective-permute-start | bytes 1572872 | tf_op jit(solution)/shard_map/while/body/eval_jaxpr/ppermute | solution.py:16
  160.7 3.4 copy-start.2
  164.1 11.9 collective-permute-start
  164.1 17.7 %collective-permute-start.1 = (f32[128,1024]{0,1:T(8,128)}, f32[128,1024]{0,1:T(8,128)}, u32[]{:S(2)}, u32[]{:S(2)}) collective-permute-start(f32[128,1024]{0,1:T(8,128)} %get-tuple-element.518), channel_id=1, source_target_pairs={{0,1},{1,2},{2,3},{3,4},{4,5},{5,6},{6,7},{7,0},{8,9},{9,10},{10,1... | collective-permute-start | bytes 1572872 | tf_op jit(solution)/shard_map/while/body/eval_jaxpr/ppermute | solution.py:16
  180.3 3.4 copy-start.2
  184.7 10.2 collective-permute-start.2
  (3 other events, 5.0 us)
Sparse Core Ops, SparseCore 0:
  220.6 1332.6 reduce-scatter.3
where the time goes:
time: 1560 us
  waiting for transfers between devices  1450 us (93%)
  local copies, waits for them, and re-layouts  42.5 us (3%)
  matrix products  32.6 us (2%)
  other arithmetic  20.6 us (1%)
    unnamed x2, waiting for transfers between devices  1330 us
    ppermute x15, waiting for transfers between devices, shifted(): return lax.ppermute(value, axis, pairs)  119 us
  transfers between devices with their start and end apart: 16, of which 16 were waited for; matrix products, arithmetic and copies ran while one was open for 2% of the time, Pallas kernels for 0%

commit v1 on v0

v1 whole, which is shorter than its diff:
```python
import math

import jax
import jax.numpy as jnp
from jax import lax
from jax.experimental import pallas as pl
from jax.experimental.pallas import tpu as pltpu
from jax.sharding import PartitionSpec as P

KV_HEADS = 4
GROUP = 8
HEADS = KV_HEADS * GROUP
HEAD = 128
ROWS = 128
CTX = 8
DP = 32
Z = 8
OUT_ROWS = 16
KEYS = 256
SCALE = 1.0 / math.sqrt(HEAD)
LOG2E = math.log2(math.e)
MESH = pl.DeviceIdType.MESH
F32, BF16 = jnp.float32, jnp.bfloat16


def wait_for(ref, sem):
    pltpu.make_async_copy(ref, ref, sem).wait()


def dot(a, b, contract):
    return lax.dot_general(a, b, ((contract[:1], contract[1:]), ((), ())), preferred_element_type=F32)


def kernel(
    x_in, q_in, k_in, v_in, o_in, lse_in, do_in, len_in,
    dq_out, kw_out, vw_out,
    lens, lse, delta, q, do, o, x, xt, xall, kv, bias, pt, dst, dqt, part, parts, grads, w,
    c_land, acc, y_out, y_land, z_out, z_land,
    in_sem, kv_send, kv_recv, x_send, x_recv, p_send, p_recv, g_send, g_recv, d_send, d_recv,
):
    dp, ctx = lax.axis_index("dp"), lax.axis_index("ctx")
    y_hi, cx = ctx // 4, ctx % 4
    y_lo, z, core = dp // (2 * Z), dp // 2 % Z, dp % 2

    def ahead(s):
        return (y_hi + s // 4) % 2 * 4 + (cx + s % 4) % 4

    def behind(s):
        return (y_hi + 2 - s // 4) % 2 * 4 + (cx + 4 - s % 4) % 4

    def z_peer(s):
        return (y_lo * Z + (z + s) % Z) * 2 + core

    core_peer = (y_lo * Z + z) * 2 + 1 - core
    y_peer = ((1 - y_lo) * Z + z) * 2 + core

    def remote(src, dst, send, recv, to):
        return pltpu.make_async_remote_copy(src, dst, send, recv, device_id=to, device_id_type=MESH)

    def cols(h):
        return pl.ds(pl.multiple_of(h * HEAD, HEAD), HEAD)

    pltpu.make_async_copy(len_in, lens, in_sem.at[0]).start()
    pltpu.make_async_copy(lse_in, lse, in_sem.at[1]).start()
    pltpu.make_async_copy(x_in, x, in_sem.at[5]).start()
    pltpu.make_async_copy(o_in, o, in_sem.at[4]).start()

    @pl.loop(0, HEADS)
    def _(h):
        pltpu.make_async_copy(do_in.at[:, cols(h)], do.at[h], in_sem.at[3]).start()
        pltpu.make_async_copy(q_in.at[:, cols(h)], q.at[h], in_sem.at[2]).start()

    @pl.loop(0, KV_HEADS)
    def _(g):
        pltpu.make_async_copy(k_in.at[:, cols(g)], kv.at[g, 0, 0], in_sem.at[6]).start()
        pltpu.make_async_copy(v_in.at[:, cols(g)], kv.at[g, 0, 1], in_sem.at[6]).start()

    barrier = pltpu.get_barrier_semaphore()

    @pl.loop(1, CTX)
    def _(s):
        pl.semaphore_signal(barrier, inc=1, device_id=(dp, ahead(s)), device_id_type=MESH)

    @pl.loop(1, Z)
    def _(s):
        pl.semaphore_signal(barrier, inc=1, device_id=(z_peer(s), ctx), device_id_type=MESH)

    for peer in (core_peer, y_peer):
        pl.semaphore_signal(barrier, inc=1, device_id=(peer, ctx), device_id_type=MESH)
    pl.semaphore_wait(barrier, CTX - 1 + Z - 1 + 2)

    wait_for(kv.at[:, 0], in_sem.at[6])

    @pl.loop(0, KV_HEADS)
    def _(g):
        @pl.loop(1, CTX)
        def _(s):
            remote(kv.at[g, 0], kv.at[g, s], kv_send, kv_recv.at[g], (dp, ahead(s))).start()

    wait_for(x, in_sem.at[5])

    @pl.loop(0, DP)
    def _(b):
        xt[b] = jnp.transpose(x[:, cols(b)]).reshape(CTX, OUT_ROWS, ROWS)

    pltpu.make_async_copy(xt.at[:, ctx], xall.at[:, :, 0:ROWS], in_sem.at[7]).start()

    @pl.loop(1, CTX)
    def _(s):
        to = ahead(s)
        remote(xt.at[:, to], xall.at[:, :, cols(s)], x_send, x_recv, (dp, to)).start()

    wait_for(lens, in_sem.at[0])
    end0 = lens[0, 0]
    end1 = end0 + lens[0, 1]
    end2 = end1 + lens[0, 2]
    end3 = end2 + lens[0, 3]
    query_pos = lax.broadcasted_iota(jnp.int32, (ROWS, ROWS), 1) * CTX + ctx
    first = jnp.zeros((ROWS, ROWS), jnp.int32)
    for end in (end0, end1, end2, end3):
        first = jnp.where(query_pos >= end, end, first)

    @pl.loop(0, CTX)
    def _(s):
        key_pos = lax.broadcasted_iota(jnp.int32, (ROWS, ROWS), 0) * CTX + behind(s)
        allowed = (key_pos >= first) & (key_pos <= query_pos)
        bias[s] = jnp.where(allowed, 0.0, -1e30).astype(F32)

    wait_for(lse, in_sem.at[1])
    wait_for(o, in_sem.at[4])
    wait_for(do, in_sem.at[3])
    wait_for(q, in_sem.at[2])

    @pl.loop(0, KV_HEADS)
    def _(g):
        rows = []
        for h in range(GROUP):
            head = g * GROUP + h
            product = do[head].astype(F32) * o[:, cols(head)].astype(F32)
            rows.append(jnp.sum(jnp.transpose(product), axis=0, keepdims=True))
        delta[pl.ds(pl.multiple_of(g * GROUP, GROUP), GROUP), :] = jnp.concatenate(rows, axis=0)

    def attend(g):
        wait_for(kv.at[g, 1:CTX], kv_recv.at[g])
        heads = pl.ds(pl.multiple_of(g * GROUP, GROUP), GROUP)
        log2_totals = lse[heads, :] * LOG2E
        deltas = delta[heads, :]
        dqt[...] = jnp.zeros_like(dqt)

        @pl.loop(0, CTX * ROWS // KEYS)
        def _(t):
            blocks = pl.ds(t * (KEYS // ROWS), KEYS // ROWS)
            keys = kv[g, blocks, 0].reshape(KEYS, HEAD)
            values = kv[g, blocks, 1].reshape(KEYS, HEAD)
            queries = q[heads].reshape(GROUP * ROWS, HEAD)
            out_grads = do[heads].reshape(GROUP * ROWS, HEAD)
            seen = bias[blocks].reshape(KEYS, ROWS)
            scores = dot(keys, queries, (1, 1))
            grad_probs = dot(values, out_grads, (1, 1))
            for h in range(GROUP):
                at = slice(h * ROWS, (h + 1) * ROWS)
                probs = jnp.exp2(scores[:, at] * (SCALE * LOG2E) + (seen - log2_totals[h : h + 1, :]))
                pt[:, at] = probs.astype(BF16)
                dst[:, at] = (probs * (grad_probs[:, at] - deltas[h : h + 1, :])).astype(BF16)
            grad_scores = dst[...]
            dv = dot(pt[...], out_grads, (1, 0))
            dk = dot(grad_scores, queries, (1, 0)) * SCALE
            part[g, blocks, :, 0:HEAD] = dk.astype(BF16).reshape(KEYS // ROWS, ROWS, HEAD)
            part[g, blocks, :, HEAD:] = dv.astype(BF16).reshape(KEYS // ROWS, ROWS, HEAD)
            dqt[...] += dot(keys, grad_scores, (0, 0))

        @pl.loop(1, CTX)
        def _(s):
            remote(part.at[g, s], parts.at[g, s], p_send, p_recv.at[g], (dp, behind(s))).start()

        for h in range(GROUP):
            block = jnp.transpose(dqt[:, h * ROWS : (h + 1) * ROWS]) * SCALE
            dq_out[:, cols(g * GROUP + h)] = block.astype(BF16)

    def gather_sums(g):
        wait_for(parts.at[g, 1:CTX], p_recv.at[g])
        total = part[g, 0].astype(F32)
        for s in range(1, CTX):
            total += parts[g, s].astype(F32)
        grads[g, 0] = total.astype(BF16)

        @pl.loop(1, CTX)
        def _(s):
            remote(grads.at[g, 0], grads.at[g, s], g_send, g_recv.at[g], (dp, ahead(s))).start()

    def weigh(g):
        wait_for(grads.at[g, 1:CTX], g_recv.at[g])
        product = dot(xall[...].reshape(DP * OUT_ROWS, CTX * ROWS), grads[g].reshape(CTX * ROWS, 2 * HEAD), (1, 0))
        at = pl.ds(pl.multiple_of(g * 2 * HEAD, 2 * HEAD), 2 * HEAD)
        w[:, :, :, :, at] = product.reshape(2, Z, 2, OUT_ROWS, 2 * HEAD)

    @pl.loop(0, KV_HEADS + 2)
    def _(step):
        @pl.when(step < KV_HEADS)
        def _():
            attend(step)

        @pl.when((step >= 1) & (step <= KV_HEADS))
        def _():
            gather_sums(step - 1)

        @pl.when(step == 2)
        def _():
            wait_for(xt.at[:, 0], in_sem.at[7])
            wait_for(xall.at[:, :, ROWS:], x_recv)

        @pl.when(step >= 2)
        def _():
            weigh(step - 2)

    to_core = remote(w.at[:, :, 1 - core], c_land, d_send.at[0], d_recv.at[0], (core_peer, ctx))
    to_core.start()
    to_core.wait()
    acc[...] = w[:, :, core] + c_land[...]
    y_out[...] = acc[1 - y_lo].astype(BF16)
    to_y = remote(y_out, y_land, d_send.at[1], d_recv.at[1], (y_peer, ctx))
    to_y.start()
    to_y.wait()
    acc[0] = acc[y_lo] + y_land[...].astype(F32)
    z_out[...] = acc[0].astype(BF16)

    @pl.loop(1, Z)
    def _(s):
        remote(z_out.at[(z + s) % Z], z_land.at[s], d_send.at[2], d_recv.at[2], (z_peer(s), ctx)).start()

    wait_for(z_land.at[1:Z], d_recv.at[2])
    total = acc[0, z]
    for s in range(1, Z):
        total += z_land[s].astype(F32)
    for g in range(KV_HEADS):
        at = slice(g * HEAD, (g + 1) * HEAD)
        kw_out[:, at] = total[:, 2 * g * HEAD : (2 * g + 1) * HEAD]
        vw_out[:, at] = total[:, (2 * g + 1) * HEAD : (2 * g + 2) * HEAD]

    wait_for(kv.at[:, 1:CTX], kv_send)
    wait_for(xall.at[:, :, ROWS:], x_send)
    wait_for(part.at[:, 1:CTX], p_send)
    wait_for(grads.at[:, 1:CTX], g_send)
    wait_for(z_land.at[1:Z], d_send.at[2])


def local(normed_input, queries, keys, values, attention_output, log_totals, output_gradient, lengths):
    dma = pltpu.SemaphoreType.DMA
    vmem = pltpu.VMEM
    return pl.pallas_call(
        kernel,
        out_shape=(
            jax.ShapeDtypeStruct((ROWS, HEADS * HEAD), BF16),
            jax.ShapeDtypeStruct((OUT_ROWS, KV_HEADS * HEAD), F32),
            jax.ShapeDtypeStruct((OUT_ROWS, KV_HEADS * HEAD), F32),
        ),
        in_specs=[pl.BlockSpec(memory_space=pl.ANY)] * 8,
        out_specs=(pl.BlockSpec(memory_space=vmem),) * 3,
        scratch_shapes=[
            pltpu.SMEM((1, 4), jnp.int32),
            vmem((HEADS, ROWS), F32),
            vmem((HEADS, ROWS), F32),
            vmem((HEADS, ROWS, HEAD), BF16),
            vmem((HEADS, ROWS, HEAD), BF16),
            vmem((ROWS, HEADS * HEAD), BF16),
            vmem((ROWS, DP * CTX * OUT_ROWS), BF16),
            vmem((DP, CTX, OUT_ROWS, ROWS), BF16),
            vmem((DP, OUT_ROWS, CTX * ROWS), BF16),
            vmem((KV_HEADS, CTX, 2, ROWS, HEAD), BF16),
            vmem((CTX, ROWS, ROWS), F32),
            vmem((KEYS, GROUP * ROWS), BF16),
            vmem((KEYS, GROUP * ROWS), BF16),
            vmem((HEAD, GROUP * ROWS), F32),
            vmem((KV_HEADS, CTX, ROWS, 2 * HEAD), BF16),
            vmem((KV_HEADS, CTX, ROWS, 2 * HEAD), BF16),
            vmem((KV_HEADS, CTX, ROWS, 2 * HEAD), BF16),
            vmem((2, Z, 2, OUT_ROWS, 2 * KV_HEADS * HEAD), F32),
            vmem((2, Z, OUT_ROWS, 2 * KV_HEADS * HEAD), F32),
            vmem((2, Z, OUT_ROWS, 2 * KV_HEADS * HEAD), F32),
            vmem((Z, OUT_ROWS, 2 * KV_HEADS * HEAD), BF16),
            vmem((Z, OUT_ROWS, 2 * KV_HEADS * HEAD), BF16),
            vmem((Z, OUT_ROWS, 2 * KV_HEADS * HEAD), BF16),
            vmem((Z, OUT_ROWS, 2 * KV_HEADS * HEAD), BF16),
            dma((8,)),
            dma,
            dma((KV_HEADS,)),
            dma,
            dma,
            dma,
            dma((KV_HEADS,)),
            dma,
            dma((KV_HEADS,)),
            dma((3,)),
            dma((3,)),
        ],
        compiler_params=pltpu.CompilerParams(
            collective_id=0, has_side_effects=True, vmem_limit_bytes=56 * 2**20
        ),
    )(normed_input, queries, keys, values, attention_output, log_totals.T, output_gradient, lengths)


def solution(mesh):
    rows = P(("dp", "ctx"), None)
    return jax.shard_map(
        local,
        mesh=mesh,
        in_specs=(rows,) * 7 + (P("dp", None),),
        out_specs=(rows, rows, rows),
        check_vma=False,
    )
```

time: 1560 us -> 117 us (0.07)
  the two profiles are of different devices: /device:TPU:128 before, /device:TPU:1 now
where the time goes in v1:
time: 117 us
  Pallas kernels  112 us (96%)
  local copies, waits for them, and re-layouts  3.68 us (3%)
    pallas_call x1, Pallas kernels, local(): pl.pallas_call(kernel, out_shape=(jax.ShapeDtypeStruct((ROWS, HEADS * HEA...  112 us
    unnamed x7, local copies, waits for them, and re-layouts  3.68 us

profile of v1, /device:TPU:1, one launch (start us, length us, event | category | flops | bytes accessed | tf_op | source)
XLA Modules:
  0.0 116.6 jit_solution(17486050648753734873)
XLA Ops:
  0.6 112.2 %shard_map.103 = (bf16[128,4096]{1,0:T(8,128)(2,1)}, f32[16,512]{1,0:T(8,128)}, f32[16,512]{1,0:T(8,128)}) custom-call(bf16[128,4096]{1,0:T(8,128)(2,1)} %x_in.1, bf16[128,4096]{1,0:T(8,128)(2,1)} %q_in.1, bf16[128,512]{1,0:T(8,128)(2,1)} %k_in.1, bf16[128,512]{1,0:T(8,128)(2,1)} %v_in.1, bf16[128,4096]{1,0:T(8,128)(2,1)} %o_in.1, f32[32,128]{1,0:T(8,128)} %bitcast.1, ...), custom_call_target="tpu_custom_call" | custom-call | tf_op jit(solution)/shard_map/pallas_call | solution.py:250
  112.9 0.0 copy-start.1
  112.9 2.3 %copy.14 = bf16[128,4096]{1,0:T(8,128)(2,1)} copy(bf16[128,4096]{1,0:T(8,128)(2,1)} %get-tuple-element.6) | data formatting | bytes 2097152
  115.2 0.0 copy-done.1
  115.2 0.0 copy-start
  115.2 0.6 copy.15
  115.8 0.2 copy-done
  115.9 0.6 copy.16
Async XLA Ops:
  112.9 2.3 %copy-start.1 = (f32[16,512]{1,0:T(8,128)S(1)}, f32[16,512]{1,0:T(8,128)}, u32[]{:S(2)}) copy-start(f32[16,512]{1,0:T(8,128)} %get-tuple-element.7) | copy-start | bytes 98308
  115.2 0.8 copy-start

commit v2 on v1

v2 whole, which is shorter than its diff:
```python
import math

import jax
import jax.numpy as jnp
from jax import lax
from jax.experimental import pallas as pl
from jax.experimental.pallas import tpu as pltpu
from jax.sharding import PartitionSpec as P

KV_HEADS = 4
GROUP = 8
HEADS = KV_HEADS * GROUP
HEAD = 128
ROWS = 128
CTX = 8
Y_FIRST = 2
DP = 32
LAGS = (1, 2, 3, 3, 4, 5)
Z = 8
OUT_ROWS = 16
KEYS = 256
SCALE = 1.0 / math.sqrt(HEAD)
LOG2E = math.log2(math.e)
MESH = pl.DeviceIdType.MESH
F32, BF16 = jnp.float32, jnp.bfloat16


def wait_for(ref, sem):
    pltpu.make_async_copy(ref, ref, sem).wait()


def dot(a, b, contract):
    return lax.dot_general(a, b, ((contract[:1], contract[1:]), ((), ())), preferred_element_type=F32)


def kernel(
    x_in, q_in, k_in, v_in, o_in, lse_in, do_in, len_in,
    dq_out, kw_out, vw_out,
    lens, lse, delta, q, do, o, x, xt, xall, kv, bias, pt, dst, dqt, part, y_parts, x_parts, mids, owned, grads, w,
    x_acc, x_out, x_land, z_acc, z_out, z_land,
    in_sem, kv_send, kv_recv, xt_send, xt_recv, p_send, p_recv, m_recv, g_send, g_recv, c_recv,
    x_send, x_recv, z_send, z_recv,
):
    dp, ctx = lax.axis_index("dp"), lax.axis_index("ctx")
    y_hi, cx = ctx // 4, ctx % 4
    y_lo, z, core = dp // (2 * Z), dp // 2 % Z, dp % 2
    y = y_hi * 2 + y_lo

    def behind(s):
        return (y_hi + s % 2) % 2 * 4 + (cx + 4 - s // 2) % 4

    y_partner = (dp, (1 - y_hi) * 4 + cx)

    def along_z(s):
        return ((y_lo * Z + (z + s) % Z) * 2 + core, ctx)

    def along_x(s):
        return (dp, y_hi * 4 + (cx + s) % 4)

    def member(s):
        return (core + s // 4) % 2, (y + s % 4) % 4

    def device(its_core, its_y):
        return ((its_y % 2 * Z + z) * 2 + its_core, its_y // 2 * 4 + cx)

    def remote(src, dst, send, recv, to):
        return pltpu.make_async_remote_copy(src, dst, send, recv, device_id=to, device_id_type=MESH)

    def cols(h):
        return pl.ds(pl.multiple_of(h * HEAD, HEAD), HEAD)

    @pl.loop(0, KV_HEADS)
    def _(g):
        pltpu.make_async_copy(k_in.at[:, cols(g)], kv.at[g, 0, 0], in_sem.at[6]).start()
        pltpu.make_async_copy(v_in.at[:, cols(g)], kv.at[g, 0, 1], in_sem.at[6]).start()

    pltpu.make_async_copy(x_in, x, in_sem.at[5]).start()
    pltpu.make_async_copy(len_in, lens, in_sem.at[0]).start()
    pltpu.make_async_copy(lse_in, lse, in_sem.at[1]).start()
    pltpu.make_async_copy(o_in, o, in_sem.at[4]).start()

    @pl.loop(0, HEADS)
    def _(h):
        pltpu.make_async_copy(do_in.at[:, cols(h)], do.at[h], in_sem.at[3]).start()
        pltpu.make_async_copy(q_in.at[:, cols(h)], q.at[h], in_sem.at[2]).start()

    barrier = pltpu.get_barrier_semaphore()

    @pl.loop(1, 8)
    def _(s):
        for to in (along_z(s), device(*member(s))):
            pl.semaphore_signal(barrier, inc=1, device_id=to, device_id_type=MESH)

    for s in range(1, 4):
        pl.semaphore_signal(barrier, inc=1, device_id=along_x(s), device_id_type=MESH)
    pl.semaphore_wait(barrier, 17)

    wait_for(kv.at[:, 0], in_sem.at[6])

    @pl.loop(0, KV_HEADS)
    def _(g):
        remote(kv.at[g, 0], kv.at[g, 1], kv_send, kv_recv.at[g, 1], y_partner).start()

    def send_along_x(g, source):
        for d in (1, 3, 2):
            remote(kv.at[g, source], kv.at[g, 2 * d + source], kv_send, kv_recv.at[g, 0], along_x(d)).start()

    def pass_on(g):
        wait_for(kv.at[g, 1], kv_recv.at[g, 1])
        send_along_x(g, 1)

    send_along_x(0, 0)
    send_along_x(1, 0)

    wait_for(x, in_sem.at[5])

    @pl.loop(0, DP)
    def _(b):
        xt[b // (2 * Z), b // 2 % Z, b % 2] = jnp.transpose(x[:, cols(b)]).reshape(2, 4, OUT_ROWS, ROWS)

    pltpu.make_async_copy(xt.at[y_lo, :, core, y_hi], xall.at[:, :, :, 0:ROWS], in_sem.at[7]).start()

    @pl.loop(1, 8)
    def _(s):
        its_core, its_y = member(s)
        mine = xt.at[its_y % 2, :, its_core, its_y // 2]
        remote(mine, xall.at[:, :, :, cols(s)], xt_send, xt_recv, device(its_core, its_y)).start()

    pass_on(0)
    send_along_x(2, 0)
    pass_on(1)
    send_along_x(3, 0)

    wait_for(lens, in_sem.at[0])
    end0 = lens[0, 0]
    end1 = end0 + lens[0, 1]
    end2 = end1 + lens[0, 2]
    end3 = end2 + lens[0, 3]
    query_pos = lax.broadcasted_iota(jnp.int32, (ROWS, ROWS), 1) * CTX + ctx
    first = jnp.zeros((ROWS, ROWS), jnp.int32)
    for end in (end0, end1, end2, end3):
        first = jnp.where(query_pos >= end, end, first)

    @pl.loop(0, CTX)
    def _(s):
        key_pos = lax.broadcasted_iota(jnp.int32, (ROWS, ROWS), 0) * CTX + behind(s)
        allowed = (key_pos >= first) & (key_pos <= query_pos)
        bias[s] = jnp.where(allowed, 0.0, -1e30).astype(F32)

    pass_on(2)
    wait_for(lse, in_sem.at[1])
    wait_for(o, in_sem.at[4])
    wait_for(do, in_sem.at[3])
    wait_for(q, in_sem.at[2])

    @pl.loop(0, KV_HEADS)
    def _(g):
        rows = []
        for h in range(GROUP):
            head = g * GROUP + h
            product = do[head].astype(F32) * o[:, cols(head)].astype(F32)
            rows.append(jnp.sum(jnp.transpose(product), axis=0, keepdims=True))
        delta[pl.ds(pl.multiple_of(g * GROUP, GROUP), GROUP), :] = jnp.concatenate(rows, axis=0)

    pass_on(3)

    def attend(g):
        wait_for(kv.at[g, 2:8], kv_recv.at[g, 0])
        heads = pl.ds(pl.multiple_of(g * GROUP, GROUP), GROUP)
        log2_totals = lse[heads, :] * LOG2E
        deltas = delta[heads, :]
        dqt[...] = jnp.zeros_like(dqt)

        @pl.loop(0, CTX * ROWS // KEYS)
        def _(t):
            blocks = pl.ds(t * (KEYS // ROWS), KEYS // ROWS)
            keys = kv[g, blocks, 0].reshape(KEYS, HEAD)
            values = kv[g, blocks, 1].reshape(KEYS, HEAD)
            queries = q[heads].reshape(GROUP * ROWS, HEAD)
            out_grads = do[heads].reshape(GROUP * ROWS, HEAD)
            seen = bias[blocks].reshape(KEYS, ROWS)
            scores = dot(keys, queries, (1, 1))
            grad_probs = dot(values, out_grads, (1, 1))
            for h in range(GROUP):
                at = slice(h * ROWS, (h + 1) * ROWS)
                probs = jnp.exp2(scores[:, at] * (SCALE * LOG2E) + (seen - log2_totals[h : h + 1, :]))
                pt[:, at] = probs.astype(BF16)
                dst[:, at] = (probs * (grad_probs[:, at] - deltas[h : h + 1, :])).astype(BF16)
            grad_scores = dst[...]
            dv = dot(pt[...], out_grads, (1, 0))
            dk = dot(grad_scores, queries, (1, 0)) * SCALE
            part[g, t, :, :, 0:HEAD] = dk.astype(BF16).reshape(2, ROWS, HEAD)
            part[g, t, :, :, HEAD:] = dv.astype(BF16).reshape(2, ROWS, HEAD)
            dqt[...] += dot(keys, grad_scores, (0, 0))

        @pl.when(g < Y_FIRST)
        def _():
            remote(part.at[g, :, 1], y_parts.at[g], p_send, p_recv.at[g], y_partner).start()

        @pl.when(g >= Y_FIRST)
        def _():
            for d in (1, 3, 2):
                remote(part.at[g, d], x_parts.at[g, d], p_send, p_recv.at[g], along_x(4 - d)).start()

        for h in range(GROUP):
            block = jnp.transpose(dqt[:, h * ROWS : (h + 1) * ROWS]) * SCALE
            dq_out[:, cols(g * GROUP + h)] = block.astype(BF16)

    def half_sums(g):
        @pl.when(g < Y_FIRST)
        def _():
            wait_for(y_parts.at[g], p_recv.at[g])
            owned[g] = part[g, 0, 0].astype(F32) + y_parts[g, 0].astype(F32)
            for d in (1, 3, 2):
                mids[g, d] = (part[g, d, 0].astype(F32) + y_parts[g, d].astype(F32)).astype(BF16)
                remote(mids.at[g, d], x_parts.at[g, d, 0], p_send, m_recv.at[g], along_x(4 - d)).start()

        @pl.when(g >= Y_FIRST)
        def _():
            wait_for(x_parts.at[g, 1:4], p_recv.at[g])
            other = part[g, 0, 1].astype(F32)
            for d in range(1, 4):
                other += x_parts[g, d, 1].astype(F32)
            mids[g, 0] = other.astype(BF16)
            remote(mids.at[g, 0], y_parts.at[g, 0], p_send, m_recv.at[g], y_partner).start()
            mine = part[g, 0, 0].astype(F32)
            for d in range(1, 4):
                mine += x_parts[g, d, 0].astype(F32)
            owned[g] = mine

    def gather_sums(g):
        @pl.when(g < Y_FIRST)
        def _():
            wait_for(x_parts.at[g, 1:4, 0], m_recv.at[g])
            total = owned[g]
            for d in range(1, 4):
                total += x_parts[g, d, 0].astype(F32)
            grads[g, 0] = total.astype(BF16)

        @pl.when(g >= Y_FIRST)
        def _():
            wait_for(y_parts.at[g, 0], m_recv.at[g])
            grads[g, 0] = (owned[g] + y_parts[g, 0].astype(F32)).astype(BF16)

        for s in range(1, 4):
            remote(grads.at[g, 0], grads.at[g, s], g_send, g_recv.at[g], device(*member(s))).start()
        remote(grads.at[g, 0], grads.at[g, 4], g_send, c_recv.at[g], device(*member(4))).start()

    def hand_over(g):
        wait_for(grads.at[g, 1:4], g_recv.at[g])
        remote(grads.at[g, 1:4], grads.at[g, 5:8], g_send, c_recv.at[g], device(*member(4))).start()

    def weigh(g):
        wait_for(grads.at[g, 4:8], c_recv.at[g])
        product = dot(xall[...].reshape(8 * 4 * OUT_ROWS, CTX * ROWS), grads[g].reshape(CTX * ROWS, 2 * HEAD), (1, 0))
        w[...] = product.reshape(Z, 4, OUT_ROWS, 2 * HEAD)
        x_out[g] = w[...].astype(BF16)
        for d in (1, 3, 2):
            to = along_x(d)
            remote(x_out.at[g, :, to[1] % 4], x_land.at[g, d], x_send, x_recv.at[g], to).start()
        x_acc[g] = w[:, cx]

    def sum_x(g):
        wait_for(x_land.at[g, 1:4], x_recv.at[g])
        total = x_acc[g]
        for d in range(1, 4):
            total += x_land[g, d].astype(F32)
        z_acc[g] = total
        z_out[g] = total.astype(BF16)

        @pl.loop(1, Z)
        def _(s):
            remote(z_out.at[g, (z + s) % Z], z_land.at[g, s], z_send, z_recv.at[g], along_z(s)).start()

    def sum_z(g):
        wait_for(z_land.at[g, 1:Z], z_recv.at[g])
        total = z_acc[g, z]
        for s in range(1, Z):
            total += z_land[g, s].astype(F32)
        kw_out[:, cols(g)] = total[:, 0:HEAD]
        vw_out[:, cols(g)] = total[:, HEAD:]

    stages = tuple(zip((sum_z, sum_x, hand_over, weigh, gather_sums, half_sums), (LAGS[k] for k in (5, 4, 2, 3, 1, 0))))

    @pl.loop(0, KV_HEADS + LAGS[5])
    def _(step):
        @pl.when(step < KV_HEADS)
        def _():
            attend(step)

        @pl.when(step == LAGS[3])
        def _():
            wait_for(xt.at[0, :, 0, 0], in_sem.at[7])
            wait_for(xall.at[:, :, :, ROWS:], xt_recv)

        for stage, lag in stages:

            @pl.when((step >= lag) & (step < KV_HEADS + lag))
            def _(stage=stage, lag=lag):
                stage(step - lag)

    wait_for(kv.at[:, 1:CTX], kv_send)
    wait_for(xall.at[:, :, :, ROWS:], xt_send)
    wait_for(grads.at[:, 1:8], p_send)
    wait_for(grads.at[:, 1:8], g_send)
    wait_for(x_land.at[:, 1:4], x_send)
    wait_for(z_land.at[:, 1:Z], z_send)


def local(normed_input, queries, keys, values, attention_output, log_totals, output_gradient, lengths):
    dma = pltpu.SemaphoreType.DMA
    vmem = pltpu.VMEM
    anywhere = pl.BlockSpec(memory_space=pl.ANY)
    shapes = (
        jax.ShapeDtypeStruct((ROWS, HEADS * HEAD), BF16),
        jax.ShapeDtypeStruct((OUT_ROWS, KV_HEADS * HEAD), F32),
        jax.ShapeDtypeStruct((OUT_ROWS, KV_HEADS * HEAD), F32),
    )
    return pl.pallas_call(
        kernel,
        out_shape=tuple(vmem(shape.shape, shape.dtype) for shape in shapes),
        in_specs=[anywhere] * 8,
        out_specs=(pl.BlockSpec(memory_space=vmem),) * 3,
        scratch_shapes=[
            pltpu.SMEM((1, 4), jnp.int32),
            vmem((HEADS, ROWS), F32),
            vmem((HEADS, ROWS), F32),
            vmem((HEADS, ROWS, HEAD), BF16),
            vmem((HEADS, ROWS, HEAD), BF16),
            vmem((ROWS, HEADS * HEAD), BF16),
            vmem((ROWS, DP * CTX * OUT_ROWS), BF16),
            vmem((2, Z, 2, 2, 4, OUT_ROWS, ROWS), BF16),
            vmem((Z, 4, OUT_ROWS, CTX * ROWS), BF16),
            vmem((KV_HEADS, CTX, 2, ROWS, HEAD), BF16),
            vmem((CTX, ROWS, ROWS), F32),
            vmem((KEYS, GROUP * ROWS), BF16),
            vmem((KEYS, GROUP * ROWS), BF16),
            vmem((HEAD, GROUP * ROWS), F32),
            vmem((KV_HEADS, 4, 2, ROWS, 2 * HEAD), BF16),
            vmem((KV_HEADS, 4, ROWS, 2 * HEAD), BF16),
            vmem((KV_HEADS, 4, 2, ROWS, 2 * HEAD), BF16),
            vmem((KV_HEADS, 4, ROWS, 2 * HEAD), BF16),
            vmem((KV_HEADS, ROWS, 2 * HEAD), F32),
            vmem((KV_HEADS, CTX, ROWS, 2 * HEAD), BF16),
            vmem((Z, 4, OUT_ROWS, 2 * HEAD), F32),
            vmem((KV_HEADS, Z, OUT_ROWS, 2 * HEAD), F32),
            vmem((KV_HEADS, Z, 4, OUT_ROWS, 2 * HEAD), BF16),
            vmem((KV_HEADS, 4, Z, OUT_ROWS, 2 * HEAD), BF16),
            vmem((KV_HEADS, Z, OUT_ROWS, 2 * HEAD), F32),
            vmem((KV_HEADS, Z, OUT_ROWS, 2 * HEAD), BF16),
            vmem((KV_HEADS, Z, OUT_ROWS, 2 * HEAD), BF16),
            dma((8,)),
            dma,
            dma((KV_HEADS, 2)),
            dma,
            dma,
            dma,
            dma((KV_HEADS,)),
            dma((KV_HEADS,)),
            dma,
            dma((KV_HEADS,)),
            dma((KV_HEADS,)),
            dma,
            dma((KV_HEADS,)),
            dma,
            dma((KV_HEADS,)),
        ],
        compiler_params=pltpu.CompilerParams(
            collective_id=0, has_side_effects=True, vmem_limit_bytes=56 * 2**20
        ),
    )(normed_input, queries, keys, values, attention_output, log_totals.T, output_gradient, lengths)

def solution(mesh):
    rows = P(("dp", "ctx"), None)
    return jax.shard_map(
        local,
        mesh=mesh,
        in_specs=(rows,) * 7 + (P("dp", None),),
        out_specs=(rows, rows, rows),
        check_vma=False,
    )
```

time: 117 us -> 87.3 us (0.75)
  Pallas kernels: 112 us -> 84.4 us
  local copies, waits for them, and re-layouts: 3.68 us -> 2.2 us
    pallas_call x1, Pallas kernels: 112 us -> 84.4 us  [local(): pl.pallas_call(kernel, out_shape=tuple((vmem(shape.shape, shape.dtype) fo...]
    unnamed x7 -> x3, local copies, waits for them, and re-layouts: 3.68 us -> 2.2 us
where the time goes in v2:
time: 87.3 us; the launch traced here: 87.2 us
  Pallas kernels  84.4 us (97%)
  local copies, waits for them, and re-layouts  2.2 us (3%)
    pallas_call x1, Pallas kernels, local(): pl.pallas_call(kernel, out_shape=tuple((vmem(shape.shape, shape.dtype) fo...  84.4 us
    unnamed x3, local copies, waits for them, and re-layouts  2.2 us

profile of v2, /device:TPU:1, one launch (start us, length us, event | category | flops | bytes accessed | tf_op | source)
XLA Modules:
  0.0 87.2 jit_solution(13144564166046151753)
XLA Ops:
  0.6 84.4 %shard_map.103 = (bf16[128,4096]{1,0:T(8,128)(2,1)S(1)}, f32[16,512]{1,0:T(8,128)S(1)}, f32[16,512]{1,0:T(8,128)S(1)}) custom-call(bf16[128,4096]{1,0:T(8,128)(2,1)} %x_in.1, bf16[128,4096]{1,0:T(8,128)(2,1)} %q_in.1, bf16[128,512]{1,0:T(8,128)(2,1)} %k_in.1, bf16[128,512]{1,0:T(8,128)(2,1)} %v_in.1, bf16[128,4096]{1,0:T(8,128)(2,1)} %o_in.1, ...), custom_call_target="tpu_custom_call" | custom-call | tf_op jit(solution)/shard_map/pallas_call | solution.py:319
  85.0 1.0 %copy.14 = bf16[128,4096]{1,0:T(8,128)(2,1)} copy(bf16[128,4096]{1,0:T(8,128)(2,1)S(1)} %get-tuple-element.3) | data formatting | bytes 2097152
  86.0 0.6 copy.15
  86.6 0.6 copy.16

commit v3 on v2

--- a/solution.py
+++ b/solution.py
@@ -13,9 +13,8 @@
 HEAD = 128
 ROWS = 128
 CTX = 8
-Y_FIRST = 2
 DP = 32
-LAGS = (1, 2, 3, 3, 4, 5)
+LAGS = (1, 2, 3, 3, 4)
 Z = 8
 OUT_ROWS = 16
 KEYS = 256
@@ -101,16 +100,22 @@
     def _(g):
         remote(kv.at[g, 0], kv.at[g, 1], kv_send, kv_recv.at[g, 1], y_partner).start()
 
-    def send_along_x(g, source):
-        for d in (1, 3, 2):
-            remote(kv.at[g, source], kv.at[g, 2 * d + source], kv_send, kv_recv.at[g, 0], along_x(d)).start()
-
-    def pass_on(g):
+    def to_neighbours(g, source):
+        remote(kv.at[g, source], kv.at[g, 2 + source], kv_send, kv_recv.at[g, 2], along_x(1)).start()
+        remote(kv.at[g, source], kv.at[g, 6 + source], kv_send, kv_recv.at[g, 3], along_x(3)).start()
+
+    def pass_partner(g):
         wait_for(kv.at[g, 1], kv_recv.at[g, 1])
-        send_along_x(g, 1)
-
-    send_along_x(0, 0)
-    send_along_x(1, 0)
+        to_neighbours(g, 1)
+
+    def pass_halves(g):
+        wait_for(kv.at[g, 2:4], kv_recv.at[g, 2])
+        remote(kv.at[g, 2:4, 0], kv.at[g, 4:6, 0], kv_send, kv_recv.at[g, 0], along_x(1)).start()
+        wait_for(kv.at[g, 6:8], kv_recv.at[g, 3])
+        remote(kv.at[g, 6:8, 1], kv.at[g, 4:6, 1], kv_send, kv_recv.at[g, 0], along_x(3)).start()
+
+    to_neighbours(0, 0)
+    to_neighbours(1, 0)
 
     wait_for(x, in_sem.at[5])
 
@@ -126,10 +131,9 @@
         mine = xt.at[its_y % 2, :, its_core, its_y // 2]
         remote(mine, xall.at[:, :, :, cols(s)], xt_send, xt_recv, device(its_core, its_y)).start()
 
-    pass_on(0)
-    send_along_x(2, 0)
-    pass_on(1)
-    send_along_x(3, 0)
+    pass_partner(0)
+    pass_partner(1)
+    to_neighbours(2, 0)
 
     wait_for(lens, in_sem.at[0])
     end0 = lens[0, 0]
@@ -147,7 +151,9 @@
         allowed = (key_pos >= first) & (key_pos <= query_pos)
         bias[s] = jnp.where(allowed, 0.0, -1e30).astype(F32)
 
-    pass_on(2)
+    pass_halves(0)
+    pass_partner(2)
+    to_neighbours(3, 0)
     wait_for(lse, in_sem.at[1])
     wait_for(o, in_sem.at[4])
     wait_for(do, in_sem.at[3])
@@ -162,10 +168,11 @@
             rows.append(jnp.sum(jnp.transpose(product), axis=0, keepdims=True))
         delta[pl.ds(pl.multiple_of(g * GROUP, GROUP), GROUP), :] = jnp.concatenate(rows, axis=0)
 
-    pass_on(3)
+    pass_partner(3)
+    pass_halves(1)
 
     def attend(g):
-        wait_for(kv.at[g, 2:8], kv_recv.at[g, 0])
+        wait_for(kv.at[g, 4:6], kv_recv.at[g, 0])
         heads = pl.ds(pl.multiple_of(g * GROUP, GROUP), GROUP)
         log2_totals = lse[heads, :] * LOG2E
         deltas = delta[heads, :]
@@ -193,55 +200,32 @@
             part[g, t, :, :, HEAD:] = dv.astype(BF16).reshape(2, ROWS, HEAD)
             dqt[...] += dot(keys, grad_scores, (0, 0))
 
-        @pl.when(g < Y_FIRST)
-        def _():
-            remote(part.at[g, :, 1], y_parts.at[g], p_send, p_recv.at[g], y_partner).start()
-
-        @pl.when(g >= Y_FIRST)
-        def _():
-            for d in (1, 3, 2):
-                remote(part.at[g, d], x_parts.at[g, d], p_send, p_recv.at[g], along_x(4 - d)).start()
+            @pl.when((g == 0) & (t == 1))
+            def _():
+                pass_halves(2)
+
+        for d in (1, 3, 2):
+            remote(part.at[g, d], x_parts.at[g, d], p_send, p_recv.at[g], along_x(4 - d)).start()
 
         for h in range(GROUP):
             block = jnp.transpose(dqt[:, h * ROWS : (h + 1) * ROWS]) * SCALE
             dq_out[:, cols(g * GROUP + h)] = block.astype(BF16)
 
     def half_sums(g):
-        @pl.when(g < Y_FIRST)
-        def _():
-            wait_for(y_parts.at[g], p_recv.at[g])
-            owned[g] = part[g, 0, 0].astype(F32) + y_parts[g, 0].astype(F32)
-            for d in (1, 3, 2):
-                mids[g, d] = (part[g, d, 0].astype(F32) + y_parts[g, d].astype(F32)).astype(BF16)
-                remote(mids.at[g, d], x_parts.at[g, d, 0], p_send, m_recv.at[g], along_x(4 - d)).start()
-
-        @pl.when(g >= Y_FIRST)
-        def _():
-            wait_for(x_parts.at[g, 1:4], p_recv.at[g])
-            other = part[g, 0, 1].astype(F32)
-            for d in range(1, 4):
-                other += x_parts[g, d, 1].astype(F32)
-            mids[g, 0] = other.astype(BF16)
-            remote(mids.at[g, 0], y_parts.at[g, 0], p_send, m_recv.at[g], y_partner).start()
-            mine = part[g, 0, 0].astype(F32)
-            for d in range(1, 4):
-                mine += x_parts[g, d, 0].astype(F32)
-            owned[g] = mine
+        wait_for(x_parts.at[g, 1:4], p_recv.at[g])
+        other = part[g, 0, 1].astype(F32)
+        for d in range(1, 4):
+            other += x_parts[g, d, 1].astype(F32)
+        mids[g] = other.astype(BF16)
+        remote(mids.at[g], y_parts.at[g], p_send, m_recv.at[g], y_partner).start()
+        mine = part[g, 0, 0].astype(F32)
+        for d in range(1, 4):
+            mine += x_parts[g, d, 0].astype(F32)
+        owned[g] = mine
 
     def gather_sums(g):
-        @pl.when(g < Y_FIRST)
-        def _():
-            wait_for(x_parts.at[g, 1:4, 0], m_recv.at[g])
-            total = owned[g]
-            for d in range(1, 4):
-                total += x_parts[g, d, 0].astype(F32)
-            grads[g, 0] = total.astype(BF16)
-
-        @pl.when(g >= Y_FIRST)
-        def _():
-            wait_for(y_parts.at[g, 0], m_recv.at[g])
-            grads[g, 0] = (owned[g] + y_parts[g, 0].astype(F32)).astype(BF16)
-
+        wait_for(y_parts.at[g], m_recv.at[g])
+        grads[g, 0] = (owned[g] + y_parts[g].astype(F32)).astype(BF16)
         for s in range(1, 4):
             remote(grads.at[g, 0], grads.at[g, s], g_send, g_recv.at[g], device(*member(s))).start()
         remote(grads.at[g, 0], grads.at[g, 4], g_send, c_recv.at[g], device(*member(4))).start()
@@ -280,10 +264,14 @@
         kw_out[:, cols(g)] = total[:, 0:HEAD]
         vw_out[:, cols(g)] = total[:, HEAD:]
 
-    stages = tuple(zip((sum_z, sum_x, hand_over, weigh, gather_sums, half_sums), (LAGS[k] for k in (5, 4, 2, 3, 1, 0))))
-
-    @pl.loop(0, KV_HEADS + LAGS[5])
+    stages = ((hand_over, LAGS[2]), (gather_sums, LAGS[1]), (sum_x, LAGS[4]), (weigh, LAGS[3]), (half_sums, LAGS[0]))
+
+    @pl.loop(0, KV_HEADS + LAGS[4])
     def _(step):
+        @pl.when(step == 1)
+        def _():
+            pass_halves(3)
+
         @pl.when(step < KV_HEADS)
         def _():
             attend(step)
@@ -298,6 +286,10 @@
             @pl.when((step >= lag) & (step < KV_HEADS + lag))
             def _(stage=stage, lag=lag):
                 stage(step - lag)
+
+    @pl.loop(0, KV_HEADS)
+    def _(g):
+        sum_z(g)
 
     wait_for(kv.at[:, 1:CTX], kv_send)
     wait_for(xall.at[:, :, :, ROWS:], xt_send)
@@ -337,9 +329,9 @@
             vmem((KEYS, GROUP * ROWS), BF16),
             vmem((HEAD, GROUP * ROWS), F32),
             vmem((KV_HEADS, 4, 2, ROWS, 2 * HEAD), BF16),
-            vmem((KV_HEADS, 4, ROWS, 2 * HEAD), BF16),
+            vmem((KV_HEADS, ROWS, 2 * HEAD), BF16),
             vmem((KV_HEADS, 4, 2, ROWS, 2 * HEAD), BF16),
-            vmem((KV_HEADS, 4, ROWS, 2 * HEAD), BF16),
+            vmem((KV_HEADS, ROWS, 2 * HEAD), BF16),
             vmem((KV_HEADS, ROWS, 2 * HEAD), F32),
             vmem((KV_HEADS, CTX, ROWS, 2 * HEAD), BF16),
             vmem((Z, 4, OUT_ROWS, 2 * HEAD), F32),
@@ -351,7 +343,7 @@
             vmem((KV_HEADS, Z, OUT_ROWS, 2 * HEAD), BF16),
             dma((8,)),
             dma,
-            dma((KV_HEADS, 2)),
+            dma((KV_HEADS, 4)),
             dma,
             dma,
             dma,

time: 87.3 us -> 80.5 us (0.922)
  Pallas kernels: 84.4 us -> 77.6 us
    pallas_call x1, Pallas kernels: 84.4 us -> 77.6 us  [local(): pl.pallas_call(kernel, out_shape=tuple((vmem(shape.shape, shape.dtype) fo...]
where the time goes in v3:
time: 80.5 us; the launch traced here: 80.4 us
  Pallas kernels  77.6 us (96%)
  local copies, waits for them, and re-layouts  2.2 us (3%)
    pallas_call x1, Pallas kernels, local(): pl.pallas_call(kernel, out_shape=tuple((vmem(shape.shape, shape.dtype) fo...  77.6 us
    unnamed x3, local copies, waits for them, and re-layouts  2.2 us

profile of v3, /device:TPU:1, one launch (start us, length us, event | category | flops | bytes accessed | tf_op | source)
XLA Modules:
  0.0 80.4 jit_solution(17678279263910321436)
XLA Ops:
  0.6 77.6 %shard_map.103 = (bf16[128,4096]{1,0:T(8,128)(2,1)S(1)}, f32[16,512]{1,0:T(8,128)S(1)}, f32[16,512]{1,0:T(8,128)S(1)}) custom-call(bf16[128,4096]{1,0:T(8,128)(2,1)} %x_in.1, bf16[128,4096]{1,0:T(8,128)(2,1)} %q_in.1, bf16[128,512]{1,0:T(8,128)(2,1)} %k_in.1, bf16[128,512]{1,0:T(8,128)(2,1)} %v_in.1, bf16[128,4096]{1,0:T(8,128)(2,1)} %o_in.1, ...), custom_call_target="tpu_custom_call" | custom-call | tf_op jit(solution)/shard_map/pallas_call | solution.py:311
  78.2 1.0 %copy.14 = bf16[128,4096]{1,0:T(8,128)(2,1)} copy(bf16[128,4096]{1,0:T(8,128)(2,1)S(1)} %get-tuple-element.3) | data formatting | bytes 2097152
  79.2 0.6 copy.15
  79.8 0.6 copy.16

commit v4 on v3

--- a/solution.py
+++ b/solution.py
@@ -125,12 +125,6 @@
 
     pltpu.make_async_copy(xt.at[y_lo, :, core, y_hi], xall.at[:, :, :, 0:ROWS], in_sem.at[7]).start()
 
-    @pl.loop(1, 8)
-    def _(s):
-        its_core, its_y = member(s)
-        mine = xt.at[its_y % 2, :, its_core, its_y // 2]
-        remote(mine, xall.at[:, :, :, cols(s)], xt_send, xt_recv, device(its_core, its_y)).start()
-
     pass_partner(0)
     pass_partner(1)
     to_neighbours(2, 0)
@@ -169,6 +163,13 @@
         delta[pl.ds(pl.multiple_of(g * GROUP, GROUP), GROUP), :] = jnp.concatenate(rows, axis=0)
 
     pass_partner(3)
+
+    @pl.loop(1, 8)
+    def _(s):
+        its_core, its_y = member(s)
+        mine = xt.at[its_y % 2, :, its_core, its_y // 2]
+        remote(mine, xall.at[:, :, :, cols(s)], xt_send, xt_recv, device(its_core, its_y)).start()
+
     pass_halves(1)
 
     def attend(g):
@@ -226,7 +227,7 @@
     def gather_sums(g):
         wait_for(y_parts.at[g], m_recv.at[g])
         grads[g, 0] = (owned[g] + y_parts[g].astype(F32)).astype(BF16)
-        for s in range(1, 4):
+        for s in (2, 1, 3):
             remote(grads.at[g, 0], grads.at[g, s], g_send, g_recv.at[g], device(*member(s))).start()
         remote(grads.at[g, 0], grads.at[g, 4], g_send, c_recv.at[g], device(*member(4))).start()
 
@@ -264,7 +265,7 @@
         kw_out[:, cols(g)] = total[:, 0:HEAD]
         vw_out[:, cols(g)] = total[:, HEAD:]
 
-    stages = ((hand_over, LAGS[2]), (gather_sums, LAGS[1]), (sum_x, LAGS[4]), (weigh, LAGS[3]), (half_sums, LAGS[0]))
+    stages = ((hand_over, LAGS[2]), (gather_sums, LAGS[1]), (weigh, LAGS[3]), (sum_x, LAGS[4]), (half_sums, LAGS[0]))
 
     @pl.loop(0, KV_HEADS + LAGS[4])
     def _(step):

time: 80.5 us -> 79.7 us (0.990)
  no operation moved by 1% of the time
where the time goes in v4:
time: 79.7 us
  Pallas kernels  76.8 us (96%)
  local copies, waits for them, and re-layouts  2.2 us (3%)
    pallas_call x1, Pallas kernels, local(): pl.pallas_call(kernel, out_shape=tuple((vmem(shape.shape, shape.dtype) fo...  76.8 us
    unnamed x3, local copies, waits for them, and re-layouts  2.2 us

profile of v4, /device:TPU:1, one launch (start us, length us, event | category | flops | bytes accessed | tf_op | source)
XLA Modules:
  0.0 79.7 jit_solution(18353330289963013368)
XLA Ops:
  0.6 76.8 %shard_map.103 = (bf16[128,4096]{1,0:T(8,128)(2,1)S(1)}, f32[16,512]{1,0:T(8,128)S(1)}, f32[16,512]{1,0:T(8,128)S(1)}) custom-call(bf16[128,4096]{1,0:T(8,128)(2,1)} %x_in.1, bf16[128,4096]{1,0:T(8,128)(2,1)} %q_in.1, bf16[128,512]{1,0:T(8,128)(2,1)} %k_in.1, bf16[128,512]{1,0:T(8,128)(2,1)} %v_in.1, bf16[128,4096]{1,0:T(8,128)(2,1)} %o_in.1, ...), custom_call_target="tpu_custom_call" | custom-call | tf_op jit(solution)/shard_map/pallas_call | solution.py:312
  77.5 1.0 %copy.14 = bf16[128,4096]{1,0:T(8,128)(2,1)} copy(bf16[128,4096]{1,0:T(8,128)(2,1)S(1)} %get-tuple-element.3) | data formatting | bytes 2097152
  78.4 0.6 copy.15
  79.0 0.6 copy.16

commit v5 on v4

--- a/solution.py
+++ b/solution.py
@@ -208,6 +208,7 @@
         for d in (1, 3, 2):
             remote(part.at[g, d], x_parts.at[g, d], p_send, p_recv.at[g], along_x(4 - d)).start()
 
+    def write_query_gradient(g):
         for h in range(GROUP):
             block = jnp.transpose(dqt[:, h * ROWS : (h + 1) * ROWS]) * SCALE
             dq_out[:, cols(g * GROUP + h)] = block.astype(BF16)
@@ -287,6 +288,10 @@
             @pl.when((step >= lag) & (step < KV_HEADS + lag))
             def _(stage=stage, lag=lag):
                 stage(step - lag)
+
+        @pl.when(step < KV_HEADS)
+        def _():
+            write_query_gradient(step)
 
     @pl.loop(0, KV_HEADS)
     def _(g):

time: 79.7 us -> 80 us (level)
  no operation moved by 1% of the time
where the time goes in v5:
time: 80 us; the launch traced here: 79.9 us
  Pallas kernels  77.1 us (96%)
  local copies, waits for them, and re-layouts  2.2 us (3%)
    pallas_call x1, Pallas kernels, local(): pl.pallas_call(kernel, out_shape=tuple((vmem(shape.shape, shape.dtype) fo...  77.1 us
    unnamed x3, local copies, waits for them, and re-layouts  2.2 us

profile of v5, /device:TPU:1, one launch (start us, length us, event | category | flops | bytes accessed | tf_op | source)
XLA Modules:
  0.0 79.9 jit_solution(15234313215156108705)
XLA Ops:
  0.6 77.1 %shard_map.103 = (bf16[128,4096]{1,0:T(8,128)(2,1)S(1)}, f32[16,512]{1,0:T(8,128)S(1)}, f32[16,512]{1,0:T(8,128)S(1)}) custom-call(bf16[128,4096]{1,0:T(8,128)(2,1)} %x_in.1, bf16[128,4096]{1,0:T(8,128)(2,1)} %q_in.1, bf16[128,512]{1,0:T(8,128)(2,1)} %k_in.1, bf16[128,512]{1,0:T(8,128)(2,1)} %v_in.1, bf16[128,4096]{1,0:T(8,128)(2,1)} %o_in.1, ...), custom_call_target="tpu_custom_call" | custom-call | tf_op jit(solution)/shard_map/pallas_call | solution.py:317
  77.7 1.0 %copy.14 = bf16[128,4096]{1,0:T(8,128)(2,1)} copy(bf16[128,4096]{1,0:T(8,128)(2,1)S(1)} %get-tuple-element.3) | data formatting | bytes 2097152
  78.7 0.6 copy.15
  79.3 0.6 copy.16
